TPU v7x, 512 devices: a whole 4x4x16 slice. The times are simulated.
512 devices in a mesh: tm: 16 (over z_hi, y), lat: 32 (over x, z_lo, core).
Axes of the slice: x: 4, y: 4, z: 16 (z_hi: 4, z_lo: 4; z = z_hi * 4 + z_lo), core: 2. Of those that a mesh axis runs over, the one named last changes fastest.
Arguments:
- cotangent: float32 [64, 512, 2048], P('tm', 'lat'), may hold values from -6 to 6
- iterates: float32 [3, 64, 512, 2048], P(None, 'tm', 'lat'), may hold values from -6 to 6
- range_field: float32 [512, 2048], P('lat', 'tm'), may hold values from 0.05 to 1
Outputs:
- noise_cotangent: float32 [64, 512, 2048], P('tm', 'lat')
- range_gradient: float32 [512, 2048], P('lat', 'tm')
All inputs are finite; a program needn't handle non-finite values.
Results may differ from a plain program's by a relative error of at most 0.0001.
Values sent between devices are 32-bit elements; how exact they have to be, the bound alone decides.
A program may use at most 64 MiB of HBM per device.

v0:
```python
import math
import jax
import jax.numpy as jnp
from jax import lax
from jax.sharding import PartitionSpec as P


def extended(cells, sides, width):
    for axis, dim in sides:
        count = lax.axis_size(axis)
        ends = count - 1
        head = lax.slice_in_dim(cells, 0, width, axis=dim)
        tail = lax.slice_in_dim(cells, cells.shape[dim] - width, cells.shape[dim], axis=dim)
        cells = jnp.concatenate(
            [
                lax.ppermute(tail, axis, [(i, (i + 1) % count) for i in range(ends)]),
                cells,
                lax.ppermute(head, axis, [((i + 1) % count, i) for i in range(ends)]),
            ],
            axis=dim,
        )
    return cells


def step_weights():
    centre_value = 6.525
    spread_value = 6.475
    root_order = (3, 0, 2, 1)
    return [
        1.0 / (centre_value + spread_value * math.cos(math.pi * (2 * section + 1) / 8.0))
        for section in root_order
    ]


def stencil(field, coefficient, previous, following, upper_row, lower_row):
    longitude = jnp.roll(field, 1, 2) + jnp.roll(field, -1, 2)
    return (
        (coefficient[None, :, :] + 6.0) * field
        - upper_row
        - lower_row
        - longitude
        - previous
        - following
    )


def body(cotangent, iterates, range_field):
    weights = step_weights()
    range_rows = lax.all_gather(range_field, "tm", axis=1, tiled=True)
    adjoint = cotangent
    noise_cot = weights[3] * cotangent
    gradient = jnp.zeros(range_field.shape, jnp.float32)
    for section in (3, 2, 1):
        own_cells = adjoint
        product_sum = -weights[section] * jnp.sum(own_cells * iterates[section - 1], axis=0)
        gradient = gradient + lax.psum_scatter(product_sum, "tm", scatter_dimension=1, tiled=True)
        timed = extended(adjoint, (("tm", 0),), 1)
        rowed = extended(adjoint, (("lat", 1),), 1)
        applied = stencil(adjoint, range_rows, timed[:-2], timed[2:], rowed[:, 2:], rowed[:, :-2])
        adjoint = adjoint - weights[section] * applied
        noise_cot = noise_cot + weights[section - 1] * adjoint
    return (noise_cot, gradient)


def solution(mesh):
    placed = (P("tm", "lat", None), P(None, "tm", "lat", None), P("lat", "tm"))
    return jax.shard_map(
        body,
        mesh=mesh,
        in_specs=placed,
        out_specs=(P("tm", "lat", None), P("lat", "tm")),
        check_vma=False,
    )
```

profile of v0, /device:TPU:4, one launch (start us, length us, event | category | flops | bytes accessed | tf_op | source)
XLA Modules:
  0.0 247.6 jit_solution(584649050877484398)
XLA Ops:
  7.2 0.0 copy-start
  7.2 0.0 copy-start.2
  7.2 0.0 reduce-scatter.2.cloned.1.call-start
  7.2 1.1 fusion.37
  8.4 5.9 %collective-permute-start = (f32[4,1,2048]{2,1,0:T(1,128)S(1)}, f32[4,1,2048]{2,1,0:T(1,128)S(1)}, u32[]{:S(2)}, u32[]{:S(2)}) collective-permute-start(f32[4,1,2048]{2,1,0:T(1,128)S(1)} %get-tuple-element.26), channel_id=1, source_target_pairs={{1,0},{2,1},{3,2},{4,3},{5,4},{6,5},{7,6},{8,7},{9,8},{10,9},{11,1... | collective-permute-start | bytes 98312 | tf_op jit(solution)/shard_map/ppermute | solution.py:18
  14.3 1.9 collective-permute-start.1
  16.2 1.0 fusion.38
  17.2 3.5 %collective-permute-start.2 = (f32[1,16,2048]{2,1,0:T(8,128)S(1)}, f32[1,16,2048]{2,1,0:T(8,128)S(1)}, u32[]{:S(2)}, u32[]{:S(2)}) collective-permute-start(f32[1,16,2048]{2,1,0:T(8,128)S(1)} %get-tuple-element.28), channel_id=1, source_target_pairs={{0,32},{32,64},{64,96},{96,128},{128,160},{160,192},{192,224},{224... | collective-permute-start | bytes 393224 | tf_op jit(solution)/shard_map/ppermute | solution.py:16
  20.7 1.3 collective-permute-start.3
  22.0 1.4 fusion.35
  23.4 0.0 copy-done.2
  23.4 58.1 %all_gather.3 = f32[16,2048]{1,0:T(8,128)S(1)} all-gather(f32[16,128]{1,0:T(8,128)S(1)} %copy-done.2), channel_id=1, replica_groups=mesh['tm'=16,'lat'=32] {'tm'}, dimensions={1}, use_global_device_ids=true | all-gather | bytes 139264 | tf_op jit(solution)/shard_map/all_gather | solution.py:49
  81.6 0.0 copy-done
  81.6 0.1 fusion.36
  81.7 0.0 collective-permute-done
  81.7 0.0 collective-permute-done.1
  81.7 0.0 collective-permute-done.2
  81.7 0.0 collective-permute-done.3
  81.7 0.3 fusion.18
  82.0 0.0 copy-start.1
  82.1 0.2 fusion.33
  82.3 2.0 collective-permute-start.4
  84.4 2.4 collective-permute-start.5
  86.8 1.3 collective-permute-start.6
  88.1 1.3 collective-permute-start.7
  89.4 0.1 fusion.32
  89.5 0.0 collective-permute-done.4
  89.5 2.8 %collective-permute-done.5 = f32[4,1,2048]{2,1,0:T(1,128)S(1)} collective-permute-done((f32[4,1,2048]{2,1,0:T(1,128)S(1)}, f32[4,1,2048]{2,1,0:T(1,128)S(1)}, u32[]{:S(2)}, u32[]{:S(2)}) %collective-permute-start.5) | collective-permute-done | bytes 32800 | tf_op jit(solution)/shard_map/ppermute | solution.py:16
  92.3 0.0 collective-permute-done.6
  92.3 3.1 %collective-permute-done.7 = f32[1,16,2048]{2,1,0:T(8,128)S(1)} collective-permute-done((f32[1,16,2048]{2,1,0:T(8,128)S(1)}, f32[1,16,2048]{2,1,0:T(8,128)S(1)}, u32[]{:S(2)}, u32[]{:S(2)}) %collective-permute-start.7) | collective-permute-done | bytes 131104 | tf_op jit(solution)/shard_map/ppermute | solution.py:18
  95.4 0.0 copy-done.1
  95.4 0.5 fusion.25
  96.0 0.2 fusion.27
  96.2 4.3 %collective-permute-start.8 = (f32[4,1,2048]{2,1,0:T(1,128)S(1)}, f32[4,1,2048]{2,1,0:T(1,128)S(1)}, u32[]{:S(2)}, u32[]{:S(2)}) collective-permute-start(f32[4,1,2048]{2,1,0:T(1,128)S(1)} %get-tuple-element.10), channel_id=1, source_target_pairs={{1,0},{2,1},{3,2},{4,3},{5,4},{6,5},{7,6},{8,7},{9,8},{10,9},{11,1... | collective-permute-start | bytes 98312 | tf_op jit(solution)/shard_map/ppermute | solution.py:18
  100.5 1.9 collective-permute-start.9
  102.4 4.9 %collective-permute-start.10 = (f32[1,16,2048]{2,1,0:T(8,128)S(1)}, f32[1,16,2048]{2,1,0:T(8,128)S(1)}, u32[]{:S(2)}, u32[]{:S(2)}) collective-permute-start(f32[1,16,2048]{2,1,0:T(8,128)S(1)} %get-tuple-element.12), channel_id=1, source_target_pairs={{0,32},{32,64},{64,96},{96,128},{128,160},{160,192},{192,224},{224... | collective-permute-start | bytes 393224 | tf_op jit(solution)/shard_map/ppermute | solution.py:16
  107.3 1.3 collective-permute-start.11
  108.6 0.7 add_add_fusion
  109.3 0.1 fusion.28
  109.4 0.0 reduce-scatter.2.cloned.1.call-update
  109.4 0.0 collective-permute-done.8
  109.4 4.2 %collective-permute-done.9 = f32[4,1,2048]{2,1,0:T(1,128)S(1)} collective-permute-done((f32[4,1,2048]{2,1,0:T(1,128)S(1)}, f32[4,1,2048]{2,1,0:T(1,128)S(1)}, u32[]{:S(2)}, u32[]{:S(2)}) %collective-permute-start.9) | collective-permute-done | bytes 32800 | tf_op jit(solution)/shard_map/ppermute | solution.py:16
  113.6 0.0 collective-permute-done.10
  113.6 6.9 %collective-permute-done.11 = f32[1,16,2048]{2,1,0:T(8,128)S(1)} collective-permute-done((f32[1,16,2048]{2,1,0:T(8,128)S(1)}, f32[1,16,2048]{2,1,0:T(8,128)S(1)}, u32[]{:S(2)}, u32[]{:S(2)}) %collective-permute-start.11) | collective-permute-done | bytes 131104 | tf_op jit(solution)/shard_map/ppermute | solution.py:18
  120.5 1.2 fusion.4
  121.7 119.0 %reduce-scatter.2.cloned.1.call-done = f32[16,128]{1,0:T(8,128)} async-done(((f32[16,2048]{1,0:T(8,128)}), f32[16,128]{1,0:T(8,128)}) %reduce-scatter.2.cloned.1.call-update) | async-done | bytes 8208 | tf_op jit(solution)/shard_map/reduce_scatter | solution.py:56
  (5 shorter events, 0.1 us)
Async XLA Ops:
  7.2 74.4 %copy-start = (f32[4,16,2048]{2,1,0:T(8,128)S(1)}, f32[4,16,2048]{2,1,0:T(8,128)}, u32[]{:S(2)}) copy-start(f32[4,16,2048]{2,1,0:T(8,128)} %param.3) | copy-start | bytes 1572868
  7.2 16.3 %copy-start.2 = (f32[16,128]{1,0:T(8,128)S(1)}, f32[16,128]{1,0:T(8,128)}, u32[]{:S(2)}) copy-start(f32[16,128]{1,0:T(8,128)} %param.5) | copy-start | bytes 24580
  7.2 233.5 %reduce-scatter.2.cloned.1.call-start = ((), (), s32[]{:S(2)}) async-start(), calls=%async_computation.1 | async-start | bytes 139264 | tf_op jit(solution)/shard_map/reduce_scatter | solution.py:56
  8.4 73.3 %collective-permute-start = (f32[4,1,2048]{2,1,0:T(1,128)S(1)}, f32[4,1,2048]{2,1,0:T(1,128)S(1)}, u32[]{:S(2)}, u32[]{:S(2)}) collective-permute-start(f32[4,1,2048]{2,1,0:T(1,128)S(1)} %get-tuple-element.26), channel_id=1, source_target_pairs={{1,0},{2,1},{3,2},{4,3},{5,4},{6,5},{7,6},{8,7},{9,8},{10,9},{11,1... | collective-permute-start | bytes 98312 | tf_op jit(solution)/shard_map/ppermute | solution.py:18
  14.3 67.3 %collective-permute-start.1 = (f32[4,1,2048]{2,1,0:T(1,128)S(1)}, f32[4,1,2048]{2,1,0:T(1,128)S(1)}, u32[]{:S(2)}, u32[]{:S(2)}) collective-permute-start(f32[4,1,2048]{2,1,0:T(1,128)S(1)} %get-tuple-element.27), channel_id=1, source_target_pairs={{0,1},{1,2},{2,3},{3,4},{4,5},{5,6},{6,7},{7,8},{8,9},{9,10},{10,1... | collective-permute-start | bytes 98312 | tf_op jit(solution)/shard_map/ppermute | solution.py:16
  17.2 64.4 %collective-permute-start.2 = (f32[1,16,2048]{2,1,0:T(8,128)S(1)}, f32[1,16,2048]{2,1,0:T(8,128)S(1)}, u32[]{:S(2)}, u32[]{:S(2)}) collective-permute-start(f32[1,16,2048]{2,1,0:T(8,128)S(1)} %get-tuple-element.28), channel_id=1, source_target_pairs={{0,32},{32,64},{64,96},{96,128},{128,160},{160,192},{192,224},{224... | collective-permute-start | bytes 393224 | tf_op jit(solution)/shard_map/ppermute | solution.py:16
  20.7 60.9 %collective-permute-start.3 = (f32[1,16,2048]{2,1,0:T(8,128)S(1)}, f32[1,16,2048]{2,1,0:T(8,128)S(1)}, u32[]{:S(2)}, u32[]{:S(2)}) collective-permute-start(f32[1,16,2048]{2,1,0:T(8,128)S(1)} %get-tuple-element.29), channel_id=1, source_target_pairs={{32,0},{64,32},{96,64},{128,96},{160,128},{192,160},{224,192},{256... | collective-permute-start | bytes 393224 | tf_op jit(solution)/shard_map/ppermute | solution.py:18
  82.0 13.4 %copy-start.1 = (f32[3,4,16,2048]{3,2,1,0:T(8,128)S(1)}, f32[3,4,16,2048]{3,2,1,0:T(8,128)}, u32[]{:S(2)}) copy-start(f32[3,4,16,2048]{3,2,1,0:T(8,128)} %param.4) | copy-start | bytes 4718596
  82.3 7.2 %collective-permute-start.4 = (f32[4,1,2048]{2,1,0:T(1,128)S(1)}, f32[4,1,2048]{2,1,0:T(1,128)S(1)}, u32[]{:S(2)}, u32[]{:S(2)}) collective-permute-start(f32[4,1,2048]{2,1,0:T(1,128)S(1)} %get-tuple-element.14), channel_id=1, source_target_pairs={{1,0},{2,1},{3,2},{4,3},{5,4},{6,5},{7,6},{8,7},{9,8},{10,9},{11,1... | collective-permute-start | bytes 98312 | tf_op jit(solution)/shard_map/ppermute | solution.py:18
  84.4 7.9 %collective-permute-start.5 = (f32[4,1,2048]{2,1,0:T(1,128)S(1)}, f32[4,1,2048]{2,1,0:T(1,128)S(1)}, u32[]{:S(2)}, u32[]{:S(2)}) collective-permute-start(f32[4,1,2048]{2,1,0:T(1,128)S(1)} %get-tuple-element.15), channel_id=1, source_target_pairs={{0,1},{1,2},{2,3},{3,4},{4,5},{5,6},{6,7},{7,8},{8,9},{9,10},{10,1... | collective-permute-start | bytes 98312 | tf_op jit(solution)/shard_map/ppermute | solution.py:16
  86.8 5.5 %collective-permute-start.6 = (f32[1,16,2048]{2,1,0:T(8,128)S(1)}, f32[1,16,2048]{2,1,0:T(8,128)S(1)}, u32[]{:S(2)}, u32[]{:S(2)}) collective-permute-start(f32[1,16,2048]{2,1,0:T(8,128)S(1)} %get-tuple-element.20), channel_id=1, source_target_pairs={{0,32},{32,64},{64,96},{96,128},{128,160},{160,192},{192,224},{224... | collective-permute-start | bytes 393224 | tf_op jit(solution)/shard_map/ppermute | solution.py:16
  88.1 7.3 %collective-permute-start.7 = (f32[1,16,2048]{2,1,0:T(8,128)S(1)}, f32[1,16,2048]{2,1,0:T(8,128)S(1)}, u32[]{:S(2)}, u32[]{:S(2)}) collective-permute-start(f32[1,16,2048]{2,1,0:T(8,128)S(1)} %get-tuple-element.21), channel_id=1, source_target_pairs={{32,0},{64,32},{96,64},{128,96},{160,128},{192,160},{224,192},{256... | collective-permute-start | bytes 393224 | tf_op jit(solution)/shard_map/ppermute | solution.py:18
  96.2 13.2 %collective-permute-start.8 = (f32[4,1,2048]{2,1,0:T(1,128)S(1)}, f32[4,1,2048]{2,1,0:T(1,128)S(1)}, u32[]{:S(2)}, u32[]{:S(2)}) collective-permute-start(f32[4,1,2048]{2,1,0:T(1,128)S(1)} %get-tuple-element.10), channel_id=1, source_target_pairs={{1,0},{2,1},{3,2},{4,3},{5,4},{6,5},{7,6},{8,7},{9,8},{10,9},{11,1... | collective-permute-start | bytes 98312 | tf_op jit(solution)/shard_map/ppermute | solution.py:18
  100.5 13.1 %collective-permute-start.9 = (f32[4,1,2048]{2,1,0:T(1,128)S(1)}, f32[4,1,2048]{2,1,0:T(1,128)S(1)}, u32[]{:S(2)}, u32[]{:S(2)}) collective-permute-start(f32[4,1,2048]{2,1,0:T(1,128)S(1)} %get-tuple-element.11), channel_id=1, source_target_pairs={{0,1},{1,2},{2,3},{3,4},{4,5},{5,6},{6,7},{7,8},{8,9},{9,10},{10,1... | collective-permute-start | bytes 98312 | tf_op jit(solution)/shard_map/ppermute | solution.py:16
  102.4 11.2 %collective-permute-start.10 = (f32[1,16,2048]{2,1,0:T(8,128)S(1)}, f32[1,16,2048]{2,1,0:T(8,128)S(1)}, u32[]{:S(2)}, u32[]{:S(2)}) collective-permute-start(f32[1,16,2048]{2,1,0:T(8,128)S(1)} %get-tuple-element.12), channel_id=1, source_target_pairs={{0,32},{32,64},{64,96},{96,128},{128,160},{160,192},{192,224},{224... | collective-permute-start | bytes 393224 | tf_op jit(solution)/shard_map/ppermute | solution.py:16
  107.3 13.1 %collective-permute-start.11 = (f32[1,16,2048]{2,1,0:T(8,128)S(1)}, f32[1,16,2048]{2,1,0:T(8,128)S(1)}, u32[]{:S(2)}, u32[]{:S(2)}) collective-permute-start(f32[1,16,2048]{2,1,0:T(8,128)S(1)} %get-tuple-element.13), channel_id=1, source_target_pairs={{32,0},{64,32},{96,64},{128,96},{160,128},{192,160},{224,192},{256... | collective-permute-start | bytes 393224 | tf_op jit(solution)/shard_map/ppermute | solution.py:18
Sparse Core Ops, SparseCore 0:
  109.6 131.1 reduce-scatter.1
where the time goes:
time: 248 us
  waiting for transfers between devices  136 us (55%)
  blocking collectives  58.1 us (23%)
  starting transfers between devices  32.1 us (13%)
  between operations  14.2 us (6%)
  local copies, waits for them, and re-layouts  4.31 us (2%)
  other arithmetic  2.77 us (1%)
    reduce_scatter x1, waiting for transfers between devices, body(): lax.psum_scatter(product_sum, 'tm', scatter_dimension=1, tiled=True)  119 us
    all_gather x1, blocking collectives, body(): range_rows = lax.all_gather(range_field, 'tm', axis=1, tiled=True)  58.1 us
    ppermute x6, starting transfers between devices, extended(): lax.ppermute(head, axis, [((i + 1) % count, i) for i in range(ends)])  16.1 us
    ppermute x6, starting transfers between devices, extended(): lax.ppermute(tail, axis, [(i, (i + 1) % count) for i in range(ends)])  16 us
    ppermute x6, waiting for transfers between devices, extended(): lax.ppermute(head, axis, [((i + 1) % count, i) for i in range(ends)])  9.98 us
    ppermute x6, waiting for transfers between devices, extended(): lax.ppermute(tail, axis, [(i, (i + 1) % count) for i in range(ends)])  7.01 us
  transfers between devices with their start and end apart: 13, of which 5 were waited for; matrix products, arithmetic and copies ran while one was open for 2% of the time, Pallas kernels for 0%

commit v1 on v0

--- a/solution.py
+++ b/solution.py
@@ -46,7 +46,9 @@
 
 def body(cotangent, iterates, range_field):
     weights = step_weights()
-    range_rows = lax.all_gather(range_field, "tm", axis=1, tiled=True)
+    range_rows = jnp.concatenate(
+        lax.all_to_all(jnp.stack([range_field] * lax.axis_size("tm")), "tm", 0, 0), axis=1
+    )
     adjoint = cotangent
     noise_cot = weights[3] * cotangent
     gradient = jnp.zeros(range_field.shape, jnp.float32)

time: 248 us -> 219 us (0.88)
  the two profiles are of different devices: /device:TPU:4 before, /device:TPU:2 now
where the time goes in v1:
time: 219 us
  waiting for transfers between devices  137 us (63%)
  starting transfers between devices  59.6 us (27%)
  between operations  14.2 us (6%)
  local copies, waits for them, and re-layouts  5.25 us (2%)
  other arithmetic  2.75 us (1%)
    reduce_scatter x1, waiting for transfers between devices, body(): lax.psum_scatter(product_sum, 'tm', scatter_dimension=1, tiled=True)  116 us
    ppermute x6, starting transfers between devices, extended(): lax.ppermute(tail, axis, [(i, (i + 1) % count) for i in range(ends)])  27.3 us
    ppermute x6, starting transfers between devices, extended(): lax.ppermute(head, axis, [((i + 1) % count, i) for i in range(ends)])  17.1 us
    all_to_all x1, starting transfers between devices, body(): lax.all_to_all(jnp.stack([range_field] * lax.axis_size('tm')), 'tm', 0, 0)  15.1 us
    all_to_all x1, waiting for transfers between devices, body(): lax.all_to_all(jnp.stack([range_field] * lax.axis_size('tm')), 'tm', 0, 0)  9.93 us
    ppermute x6, waiting for transfers between devices, extended(): lax.ppermute(head, axis, [((i + 1) % count, i) for i in range(ends)])  6.87 us
  transfers between devices with their start and end apart: 14, of which 6 were waited for; matrix products, arithmetic and copies ran while one was open for 3% of the time, Pallas kernels for 0%

profile of v1, /device:TPU:2, one launch (start us, length us, event | category | flops | bytes accessed | tf_op | source)
XLA Modules:
  0.0 218.6 jit_solution(6123142182191183341)
XLA Ops:
  7.2 0.0 copy-start
  7.2 1.1 fusion.37
  8.3 5.9 %collective-permute-start = (f32[4,1,2048]{2,1,0:T(1,128)S(1)}, f32[4,1,2048]{2,1,0:T(1,128)S(1)}, u32[]{:S(2)}, u32[]{:S(2)}) collective-permute-start(f32[4,1,2048]{2,1,0:T(1,128)S(1)} %get-tuple-element.26), channel_id=1, source_target_pairs={{1,0},{2,1},{3,2},{4,3},{5,4},{6,5},{7,6},{8,7},{9,8},{10,9},{11,1... | collective-permute-start | bytes 98312 | tf_op jit(solution)/shard_map/ppermute | solution.py:18
  14.3 1.9 collective-permute-start.1
  16.2 1.4 stack.2
  17.6 15.1 %all-to-all-start = ((f32[16,16,128]{2,1,0:T(8,128)}), f32[16,16,128]{2,1,0:T(8,128)S(1)}, u32[]{:S(2)}, u32[]{:S(2)}) async-start(f32[16,16,128]{2,1,0:T(8,128)} %stack.2), calls=%async_computation | async-start | bytes 262144 | tf_op jit(solution)/shard_map/all_to_all | solution.py:50
  32.7 0.0 reduce-scatter.2.cloned.1.call-start
  32.7 1.0 fusion.38
  33.7 3.8 %collective-permute-start.2 = (f32[1,16,2048]{2,1,0:T(8,128)S(1)}, f32[1,16,2048]{2,1,0:T(8,128)S(1)}, u32[]{:S(2)}, u32[]{:S(2)}) collective-permute-start(f32[1,16,2048]{2,1,0:T(8,128)S(1)} %get-tuple-element.28), channel_id=1, source_target_pairs={{0,32},{32,64},{64,96},{96,128},{128,160},{160,192},{192,224},{224... | collective-permute-start | bytes 393224 | tf_op jit(solution)/shard_map/ppermute | solution.py:16
  37.6 1.3 collective-permute-start.3
  38.9 0.9 fusion.36
  39.7 0.0 copy-done
  39.7 0.2 fusion.35
  39.9 9.9 %all-to-all-done = f32[16,16,128]{2,1,0:T(8,128)S(1)} async-done(((f32[16,16,128]{2,1,0:T(8,128)}), f32[16,16,128]{2,1,0:T(8,128)S(1)}, u32[]{:S(2)}, u32[]{:S(2)}) %all-to-all-start) | async-done | bytes 131104 | tf_op jit(solution)/shard_map/all_to_all | solution.py:50
  49.9 0.0 collective-permute-done
  49.9 0.0 collective-permute-done.1
  49.9 0.0 collective-permute-done.2
  49.9 0.0 collective-permute-done.3
  49.9 0.3 fusion.18
  50.2 0.0 copy-start.1
  50.3 0.2 fusion.33
  50.5 3.1 %collective-permute-start.4 = (f32[4,1,2048]{2,1,0:T(1,128)S(1)}, f32[4,1,2048]{2,1,0:T(1,128)S(1)}, u32[]{:S(2)}, u32[]{:S(2)}) collective-permute-start(f32[4,1,2048]{2,1,0:T(1,128)S(1)} %get-tuple-element.14), channel_id=1, source_target_pairs={{1,0},{2,1},{3,2},{4,3},{5,4},{6,5},{7,6},{8,7},{9,8},{10,9},{11,1... | collective-permute-start | bytes 98312 | tf_op jit(solution)/shard_map/ppermute | solution.py:18
  53.6 1.9 collective-permute-start.5
  55.6 2.3 %collective-permute-start.6 = (f32[1,16,2048]{2,1,0:T(8,128)S(1)}, f32[1,16,2048]{2,1,0:T(8,128)S(1)}, u32[]{:S(2)}, u32[]{:S(2)}) collective-permute-start(f32[1,16,2048]{2,1,0:T(8,128)S(1)} %get-tuple-element.20), channel_id=1, source_target_pairs={{0,32},{32,64},{64,96},{96,128},{128,160},{160,192},{192,224},{224... | collective-permute-start | bytes 393224 | tf_op jit(solution)/shard_map/ppermute | solution.py:16
  57.8 1.3 collective-permute-start.7
  59.1 0.1 fusion.32
  59.2 0.0 collective-permute-done.4
  59.2 3.8 %collective-permute-done.5 = f32[4,1,2048]{2,1,0:T(1,128)S(1)} collective-permute-done((f32[4,1,2048]{2,1,0:T(1,128)S(1)}, f32[4,1,2048]{2,1,0:T(1,128)S(1)}, u32[]{:S(2)}, u32[]{:S(2)}) %collective-permute-start.5) | collective-permute-done | bytes 32800 | tf_op jit(solution)/shard_map/ppermute | solution.py:16
  63.0 0.0 collective-permute-done.6
  63.0 2.7 %collective-permute-done.7 = f32[1,16,2048]{2,1,0:T(8,128)S(1)} collective-permute-done((f32[1,16,2048]{2,1,0:T(8,128)S(1)}, f32[1,16,2048]{2,1,0:T(8,128)S(1)}, u32[]{:S(2)}, u32[]{:S(2)}) %collective-permute-start.7) | collective-permute-done | bytes 131104 | tf_op jit(solution)/shard_map/ppermute | solution.py:18
  65.7 0.0 copy-done.1
  65.7 0.5 fusion.25
  66.2 0.2 fusion.27
  66.4 4.2 %collective-permute-start.8 = (f32[4,1,2048]{2,1,0:T(1,128)S(1)}, f32[4,1,2048]{2,1,0:T(1,128)S(1)}, u32[]{:S(2)}, u32[]{:S(2)}) collective-permute-start(f32[4,1,2048]{2,1,0:T(1,128)S(1)} %get-tuple-element.10), channel_id=1, source_target_pairs={{1,0},{2,1},{3,2},{4,3},{5,4},{6,5},{7,6},{8,7},{9,8},{10,9},{11,1... | collective-permute-start | bytes 98312 | tf_op jit(solution)/shard_map/ppermute | solution.py:18
  70.6 1.9 collective-permute-start.9
  72.6 15.5 %collective-permute-start.10 = (f32[1,16,2048]{2,1,0:T(8,128)S(1)}, f32[1,16,2048]{2,1,0:T(8,128)S(1)}, u32[]{:S(2)}, u32[]{:S(2)}) collective-permute-start(f32[1,16,2048]{2,1,0:T(8,128)S(1)} %get-tuple-element.12), channel_id=1, source_target_pairs={{0,32},{32,64},{64,96},{96,128},{128,160},{160,192},{192,224},{224... | collective-permute-start | bytes 393224 | tf_op jit(solution)/shard_map/ppermute | solution.py:16
  88.1 1.3 collective-permute-start.11
  89.4 0.7 add_add_fusion
  90.0 0.1 fusion.28
  90.1 0.0 reduce-scatter.2.cloned.1.call-update
  90.1 0.0 collective-permute-done.8
  90.1 0.0 collective-permute-done.9
  90.2 0.6 collective-permute-done.10
  90.7 4.2 %collective-permute-done.11 = f32[1,16,2048]{2,1,0:T(8,128)S(1)} collective-permute-done((f32[1,16,2048]{2,1,0:T(8,128)S(1)}, f32[1,16,2048]{2,1,0:T(8,128)S(1)}, u32[]{:S(2)}, u32[]{:S(2)}) %collective-permute-start.11) | collective-permute-done | bytes 131104 | tf_op jit(solution)/shard_map/ppermute | solution.py:18
  94.9 1.2 fusion.4
  96.2 115.6 %reduce-scatter.2.cloned.1.call-done = f32[16,128]{1,0:T(8,128)} async-done(((f32[16,2048]{1,0:T(8,128)}), f32[16,128]{1,0:T(8,128)}) %reduce-scatter.2.cloned.1.call-update) | async-done | bytes 8208 | tf_op jit(solution)/shard_map/reduce_scatter | solution.py:58
  (5 shorter events, 0.1 us)
Async XLA Ops:
  7.2 32.6 %copy-start = (f32[4,16,2048]{2,1,0:T(8,128)S(1)}, f32[4,16,2048]{2,1,0:T(8,128)}, u32[]{:S(2)}) copy-start(f32[4,16,2048]{2,1,0:T(8,128)} %param.3) | copy-start | bytes 1572868
  8.3 41.6 %collective-permute-start = (f32[4,1,2048]{2,1,0:T(1,128)S(1)}, f32[4,1,2048]{2,1,0:T(1,128)S(1)}, u32[]{:S(2)}, u32[]{:S(2)}) collective-permute-start(f32[4,1,2048]{2,1,0:T(1,128)S(1)} %get-tuple-element.26), channel_id=1, source_target_pairs={{1,0},{2,1},{3,2},{4,3},{5,4},{6,5},{7,6},{8,7},{9,8},{10,9},{11,1... | collective-permute-start | bytes 98312 | tf_op jit(solution)/shard_map/ppermute | solution.py:18
  14.3 35.6 %collective-permute-start.1 = (f32[4,1,2048]{2,1,0:T(1,128)S(1)}, f32[4,1,2048]{2,1,0:T(1,128)S(1)}, u32[]{:S(2)}, u32[]{:S(2)}) collective-permute-start(f32[4,1,2048]{2,1,0:T(1,128)S(1)} %get-tuple-element.27), channel_id=1, source_target_pairs={{0,1},{1,2},{2,3},{3,4},{4,5},{5,6},{6,7},{7,8},{8,9},{9,10},{10,1... | collective-permute-start | bytes 98312 | tf_op jit(solution)/shard_map/ppermute | solution.py:16
  17.6 32.3 %all-to-all-start = ((f32[16,16,128]{2,1,0:T(8,128)}), f32[16,16,128]{2,1,0:T(8,128)S(1)}, u32[]{:S(2)}, u32[]{:S(2)}) async-start(f32[16,16,128]{2,1,0:T(8,128)} %stack.2), calls=%async_computation | async-start | bytes 262144 | tf_op jit(solution)/shard_map/all_to_all | solution.py:50
  32.7 179.0 %reduce-scatter.2.cloned.1.call-start = ((), (), s32[]{:S(2)}) async-start(), calls=%async_computation.2 | async-start | bytes 139264 | tf_op jit(solution)/shard_map/reduce_scatter | solution.py:58
  33.7 16.2 %collective-permute-start.2 = (f32[1,16,2048]{2,1,0:T(8,128)S(1)}, f32[1,16,2048]{2,1,0:T(8,128)S(1)}, u32[]{:S(2)}, u32[]{:S(2)}) collective-permute-start(f32[1,16,2048]{2,1,0:T(8,128)S(1)} %get-tuple-element.28), channel_id=1, source_target_pairs={{0,32},{32,64},{64,96},{96,128},{128,160},{160,192},{192,224},{224... | collective-permute-start | bytes 393224 | tf_op jit(solution)/shard_map/ppermute | solution.py:16
  37.6 12.3 %collective-permute-start.3 = (f32[1,16,2048]{2,1,0:T(8,128)S(1)}, f32[1,16,2048]{2,1,0:T(8,128)S(1)}, u32[]{:S(2)}, u32[]{:S(2)}) collective-permute-start(f32[1,16,2048]{2,1,0:T(8,128)S(1)} %get-tuple-element.29), channel_id=1, source_target_pairs={{32,0},{64,32},{96,64},{128,96},{160,128},{192,160},{224,192},{256... | collective-permute-start | bytes 393224 | tf_op jit(solution)/shard_map/ppermute | solution.py:18
  50.2 15.4 %copy-start.1 = (f32[3,4,16,2048]{3,2,1,0:T(8,128)S(1)}, f32[3,4,16,2048]{3,2,1,0:T(8,128)}, u32[]{:S(2)}) copy-start(f32[3,4,16,2048]{3,2,1,0:T(8,128)} %param.4) | copy-start | bytes 4718596
  50.5 8.7 %collective-permute-start.4 = (f32[4,1,2048]{2,1,0:T(1,128)S(1)}, f32[4,1,2048]{2,1,0:T(1,128)S(1)}, u32[]{:S(2)}, u32[]{:S(2)}) collective-permute-start(f32[4,1,2048]{2,1,0:T(1,128)S(1)} %get-tuple-element.14), channel_id=1, source_target_pairs={{1,0},{2,1},{3,2},{4,3},{5,4},{6,5},{7,6},{8,7},{9,8},{10,9},{11,1... | collective-permute-start | bytes 98312 | tf_op jit(solution)/shard_map/ppermute | solution.py:18
  53.6 9.3 %collective-permute-start.5 = (f32[4,1,2048]{2,1,0:T(1,128)S(1)}, f32[4,1,2048]{2,1,0:T(1,128)S(1)}, u32[]{:S(2)}, u32[]{:S(2)}) collective-permute-start(f32[4,1,2048]{2,1,0:T(1,128)S(1)} %get-tuple-element.15), channel_id=1, source_target_pairs={{0,1},{1,2},{2,3},{3,4},{4,5},{5,6},{6,7},{7,8},{8,9},{9,10},{10,1... | collective-permute-start | bytes 98312 | tf_op jit(solution)/shard_map/ppermute | solution.py:16
  55.6 7.4 %collective-permute-start.6 = (f32[1,16,2048]{2,1,0:T(8,128)S(1)}, f32[1,16,2048]{2,1,0:T(8,128)S(1)}, u32[]{:S(2)}, u32[]{:S(2)}) collective-permute-start(f32[1,16,2048]{2,1,0:T(8,128)S(1)} %get-tuple-element.20), channel_id=1, source_target_pairs={{0,32},{32,64},{64,96},{96,128},{128,160},{160,192},{192,224},{224... | collective-permute-start | bytes 393224 | tf_op jit(solution)/shard_map/ppermute | solution.py:16
  57.8 7.8 %collective-permute-start.7 = (f32[1,16,2048]{2,1,0:T(8,128)S(1)}, f32[1,16,2048]{2,1,0:T(8,128)S(1)}, u32[]{:S(2)}, u32[]{:S(2)}) collective-permute-start(f32[1,16,2048]{2,1,0:T(8,128)S(1)} %get-tuple-element.21), channel_id=1, source_target_pairs={{32,0},{64,32},{96,64},{128,96},{160,128},{192,160},{224,192},{256... | collective-permute-start | bytes 393224 | tf_op jit(solution)/shard_map/ppermute | solution.py:18
  66.4 23.7 %collective-permute-start.8 = (f32[4,1,2048]{2,1,0:T(1,128)S(1)}, f32[4,1,2048]{2,1,0:T(1,128)S(1)}, u32[]{:S(2)}, u32[]{:S(2)}) collective-permute-start(f32[4,1,2048]{2,1,0:T(1,128)S(1)} %get-tuple-element.10), channel_id=1, source_target_pairs={{1,0},{2,1},{3,2},{4,3},{5,4},{6,5},{7,6},{8,7},{9,8},{10,9},{11,1... | collective-permute-start | bytes 98312 | tf_op jit(solution)/shard_map/ppermute | solution.py:18
  70.6 19.5 %collective-permute-start.9 = (f32[4,1,2048]{2,1,0:T(1,128)S(1)}, f32[4,1,2048]{2,1,0:T(1,128)S(1)}, u32[]{:S(2)}, u32[]{:S(2)}) collective-permute-start(f32[4,1,2048]{2,1,0:T(1,128)S(1)} %get-tuple-element.11), channel_id=1, source_target_pairs={{0,1},{1,2},{2,3},{3,4},{4,5},{5,6},{6,7},{7,8},{8,9},{9,10},{10,1... | collective-permute-start | bytes 98312 | tf_op jit(solution)/shard_map/ppermute | solution.py:16
  72.6 18.2 %collective-permute-start.10 = (f32[1,16,2048]{2,1,0:T(8,128)S(1)}, f32[1,16,2048]{2,1,0:T(8,128)S(1)}, u32[]{:S(2)}, u32[]{:S(2)}) collective-permute-start(f32[1,16,2048]{2,1,0:T(8,128)S(1)} %get-tuple-element.12), channel_id=1, source_target_pairs={{0,32},{32,64},{64,96},{96,128},{128,160},{160,192},{192,224},{224... | collective-permute-start | bytes 393224 | tf_op jit(solution)/shard_map/ppermute | solution.py:16
  88.1 6.9 %collective-permute-start.11 = (f32[1,16,2048]{2,1,0:T(8,128)S(1)}, f32[1,16,2048]{2,1,0:T(8,128)S(1)}, u32[]{:S(2)}, u32[]{:S(2)}) collective-permute-start(f32[1,16,2048]{2,1,0:T(8,128)S(1)} %get-tuple-element.13), channel_id=1, source_target_pairs={{32,0},{64,32},{96,64},{128,96},{160,128},{192,160},{224,192},{256... | collective-permute-start | bytes 393224 | tf_op jit(solution)/shard_map/ppermute | solution.py:18
Sparse Core Ops, SparseCore 0:
  90.3 121.4 reduce-scatter.1
